TPU v7x, 512 devices: a whole 4x4x16 slice. The times are simulated.
512 devices in a mesh: section: 32 (over y, x, core), ctx: 16 (over z).
Axes of the slice: x: 4, y: 4, z: 16, core: 2. Of those that a mesh axis runs over, the one named last changes fastest.
Arguments:
- streams: bfloat16 [32, 2048, 5120], P('section', 'ctx'), may hold values from -6 to 6
- conv_weight: bfloat16 [32, 4, 5120], P('section'), may hold values from -3 to 3
- beta_logit: float32 [32, 2048, 16], P('section', 'ctx'), may hold values from -12 to 3
- gate_log: float32 [32, 2048, 8], P('section', 'ctx'), may hold values from -2 to 0
- norm_gain: float32 [32, 1024], P('section'), may hold values from 0.25 to 1.75
- w_out: bfloat16 [32, 1024, 2048], P('section', None, 'ctx'), may hold values from -0.1875 to 0.1875
Outputs:
- handed: bfloat16 [32, 2048, 2048], P('section', 'ctx')
All inputs are finite; a program needn't handle non-finite values.
Results may differ from a plain program's by a relative error of at most 0.0049.
Values may be sent and summed in bfloat16 or wider, within the bound.
A program may use at most 128 MiB of HBM per device.

v0:
```python
import jax
import jax.numpy as jnp
from jax import lax
from jax.sharding import PartitionSpec as P

HEAD_TOTAL = 8
HK = 128
STEPS = 2
CONV = 4
SPAN = 128
highest = lax.Precision.HIGHEST


def shifted(value, axis, steps):
    count = lax.axis_size(axis)
    first, last = (max(0, -steps), min(count, count - steps))
    return lax.ppermute(value, axis, [(source, source + steps) for source in range(first, last)])


def entering(value, axis, join, neutral):
    count, mine = (lax.axis_size(axis), lax.axis_index(axis))
    pieces = jax.tree.map(lambda part: lax.all_gather(part, axis), value)
    total = jax.tree.map(
        lambda part, zero: jnp.full_like(part, 0) + jnp.asarray(zero, part.dtype), value, neutral
    )

    def turn(position, total):
        longer = join(total, jax.tree.map(lambda part: part[position], pieces))
        return jax.tree.map(lambda new, old: jnp.where(position < mine, new, old), longer, total)

    return lax.fori_loop(0, count - 1, turn, total)


def passed_along(value, axis, steps):
    count = lax.axis_size(axis)
    pairs = [(source, (source + steps) % count) for source in range(count)]
    return lax.ppermute(value, axis, pairs)


def mix_taps(extended, tap_weights):
    tok_count = extended.shape[0] - tap_weights.shape[0] + 1
    summed = jnp.zeros((tok_count, extended.shape[1]), jnp.float32)
    for offset in range(tap_weights.shape[0]):
        summed = summed + tap_weights[offset].astype(jnp.float32) * extended[
            offset : offset + tok_count
        ].astype(jnp.float32)
    return jax.nn.silu(summed)


def unit_rows(vectors):
    return vectors * lax.rsqrt(jnp.sum(vectors * vectors, axis=-1, keepdims=True) + 1e-06)


def head_major(active, beta_logit, gate_log):
    tok_count = active.shape[0]
    head_width = HEAD_TOTAL * HK
    queries = unit_rows(active[:, :head_width].reshape(tok_count, HEAD_TOTAL, HK)).transpose(
        1, 0, 2
    )
    keys_all = unit_rows(
        active[:, head_width : (1 + STEPS) * head_width].reshape(tok_count, STEPS, HEAD_TOTAL, HK)
    )
    keys_all = keys_all.transpose(2, 0, 1, 3).reshape(HEAD_TOTAL, tok_count * STEPS, HK)
    values_all = active[:, (1 + STEPS) * head_width :].reshape(tok_count, STEPS, HEAD_TOTAL, HK)
    values_all = values_all.transpose(2, 0, 1, 3).reshape(HEAD_TOTAL, tok_count * STEPS, HK)
    step_size = (
        jax.nn.sigmoid(beta_logit.reshape(tok_count, STEPS, HEAD_TOTAL))
        .transpose(2, 0, 1)
        .reshape(HEAD_TOTAL, tok_count * STEPS)
    )
    opening = (lax.broadcasted_iota(jnp.int32, (1, STEPS, 1), 1) == 0).astype(gate_log.dtype)
    log_gate = (
        (gate_log[:, None, :] * opening).transpose(2, 0, 1).reshape(HEAD_TOTAL, tok_count * STEPS)
    )
    return (queries, keys_all, values_all, step_size, log_gate)


def span_terms(queries, keys_all, values_all, step_size, log_gate):
    head_count, virtual, head_dim = keys_all.shape
    blocks = virtual // SPAN
    per_block = SPAN // STEPS
    queries = queries.reshape(head_count, blocks, per_block, head_dim)
    keys_all = keys_all.reshape(head_count, blocks, SPAN, head_dim)
    values_all = values_all.reshape(head_count, blocks, SPAN, head_dim)
    step_size = step_size.reshape(head_count, blocks, SPAN)
    cumulate = jnp.cumsum(log_gate.reshape(head_count, blocks, SPAN), axis=-1)
    query_log = cumulate[..., STEPS - 1 :: STEPS]
    row_index = lax.broadcasted_iota(jnp.int32, (SPAN, SPAN), 0)
    col_index = lax.broadcasted_iota(jnp.int32, (SPAN, SPAN), 1)
    strict = col_index < row_index
    spread = cumulate[..., :, None] - cumulate[..., None, :]
    damping = jnp.where(strict, jnp.exp(jnp.where(strict, spread, 0.0)), 0.0)
    key_inner = jnp.einsum("hcid,hcjd->hcij", keys_all, keys_all, precision=highest)
    unit_lower = (
        jnp.eye(SPAN, dtype=key_inner.dtype) + step_size[..., :, None] * damping * key_inner
    )
    right_sides = jnp.concatenate(
        [step_size[..., None] * values_all, (step_size * jnp.exp(cumulate))[..., None] * keys_all],
        axis=-1,
    )
    solved = jax.scipy.linalg.solve_triangular(
        unit_lower, right_sides, lower=True, unit_diagonal=True
    )
    value_part = solved[..., :head_dim]
    key_part = solved[..., head_dim:]
    to_end = keys_all * jnp.exp(cumulate[..., -1:] - cumulate)[..., None]
    carried = jnp.exp(cumulate[..., -1])[..., None, None] * jnp.eye(head_dim, dtype=key_inner.dtype)
    carried = carried - jnp.einsum("hcid,hcie->hcde", to_end, key_part, precision=highest)
    written = jnp.einsum("hcid,hcie->hcde", to_end, value_part, precision=highest)
    query_row = lax.broadcasted_iota(jnp.int32, (per_block, SPAN), 0) * STEPS + STEPS - 1
    query_col = lax.broadcasted_iota(jnp.int32, (per_block, SPAN), 1)
    allowed = query_col <= query_row
    query_spread = query_log[..., :, None] - cumulate[..., None, :]
    query_damping = jnp.where(allowed, jnp.exp(jnp.where(allowed, query_spread, 0.0)), 0.0)
    scores = jnp.einsum("hcpd,hcid->hcpi", queries, keys_all, precision=highest) * query_damping
    direct = jnp.einsum("hcpi,hcie->hcpe", scores, value_part, precision=highest)
    reach_map = queries * jnp.exp(query_log)[..., None] - jnp.einsum(
        "hcpi,hcie->hcpe", scores, key_part, precision=highest
    )
    return (
        jnp.moveaxis(carried, 1, 0),
        jnp.moveaxis(written, 1, 0),
        jnp.moveaxis(direct, 1, 0),
        jnp.moveaxis(reach_map, 1, 0),
    )


def advance(state_now, piece_terms):
    carried, written, direct, reach_map = piece_terms
    span_out = direct + jnp.einsum("hpd,hde->hpe", reach_map, state_now, precision=highest)
    state_now = jnp.einsum("hde,hef->hdf", carried, state_now, precision=highest) + written
    return (state_now, span_out)


def normalize(outputs, norm_gain):
    tok_count = outputs.shape[0]
    inverse_rms = lax.rsqrt(jnp.mean(outputs * outputs, axis=-1, keepdims=True) + 1e-05)
    return (
        (outputs * inverse_rms * norm_gain.reshape(HEAD_TOTAL, HK))
        .reshape(tok_count, HEAD_TOTAL * HK)
        .astype(jnp.bfloat16)
    )


def combine_pairs(earlier_pair, later_pair):
    first_map, first_add = earlier_pair
    second_map, second_add = later_pair
    joined_map = jnp.einsum("hde,hef->hdf", second_map, first_map, precision=highest)
    joined_add = jnp.einsum("hde,hef->hdf", second_map, first_add, precision=highest) + second_add
    return (joined_map, joined_add)


def compose_step(carried_in, piece_terms):
    so_far, added_state = carried_in
    next_map = jnp.einsum("hde,hef->hdf", piece_terms[0], so_far, precision=highest)
    next_add = (
        jnp.einsum("hde,hef->hdf", piece_terms[0], added_state, precision=highest) + piece_terms[1]
    )
    return ((next_map, next_add), None)


def on_device(streams, conv_weight, beta_logit, gate_log, norm_gain, w_out):
    own_rows = streams[0]
    tok_count = own_rows.shape[0]
    rim_rows = shifted(own_rows[tok_count - (CONV - 1) :], "ctx", 1)
    active = mix_taps(jnp.concatenate([rim_rows, own_rows], axis=0), conv_weight[0])
    span_parts = span_terms(*head_major(active, beta_logit[0], gate_log[0]))
    identity_map = jnp.broadcast_to(jnp.eye(HK, dtype=jnp.float32), (HEAD_TOTAL, HK, HK))
    nothing = jnp.zeros((HEAD_TOTAL, HK, HK), jnp.float32)
    (total_map, total_add), _ = lax.scan(compose_step, (identity_map, nothing), span_parts)
    _, incoming = entering((total_map, total_add), "ctx", combine_pairs, (identity_map, nothing))
    _, outputs = lax.scan(advance, incoming, span_parts)
    outputs = outputs.transpose(0, 2, 1, 3).reshape(tok_count, HEAD_TOTAL, HK)
    normed = normalize(outputs, norm_gain[0])
    local_cols = w_out[0]
    mixed_rows = jnp.dot(
        normed,
        lax.all_gather(local_cols, "ctx", axis=1, tiled=True),
        preferred_element_type=jnp.float32,
    ).astype(jnp.bfloat16)
    return passed_along(mixed_rows[None], "section", 1)


def solution(mesh):
    placed = (
        P("section", "ctx", None),
        P("section", None, None),
        P("section", "ctx", None),
        P("section", "ctx", None),
        P("section", None),
        P("section", None, "ctx"),
    )
    return jax.shard_map(
        on_device, mesh=mesh, in_specs=placed, out_specs=P("section", "ctx", None), check_vma=False
    )
```

profile of v0, /device:TPU:32, one launch (start us, length us, event | category | flops | bytes accessed | tf_op | source)
XLA Modules:
  0.0 527.9 jit_solution(1281271470755481892)
XLA Ops:
  6.5 1.0 slice_bitcast_fusion.3
  7.6 3.8 collective-permute-start
  11.4 1.0 slice_convert_fusion.3
  12.4 0.8 copy.80
  14.3 0.7 divide_bitcast_fusion
  16.3 1.8 divide_multiply_fusion
  18.5 1.1 copy-done.6
  21.2 1.5 copy.89
  22.7 2.4 fusion.43
  25.1 157.9 %custom-call.4 = f32[8,2,1,128,128]{3,4,2,1,0:T(8,128)} custom-call(f32[8,2,1,128,128]{4,3,2,1,0:T(8,128)S(1)} %fusion.43), custom_call_target="InvertDiagBlocksLowerTriangular" | custom-call | tf_op jit(solution)/shard_map/jit(_solve_triangular)/vmap(vmap())/triangular_solve | solution.py:101
  183.0 1.9 broadcast_multiply_fusion
  184.9 2.0 fusion.35
  186.9 2.2 convolution_bitcast_fusion
  189.3 2.2 fusion.39
  191.7 2.9 while.40
  194.6 0.8 copy-done.2
  197.2 1.2 slice_bitcast_fusion.2
  199.0 2.1 convolution_multiply_fusion.1
  201.2 1.9 convolution_bitcast_fusion.2
  203.0 1.1 fusion.46
  204.1 97.6 %all-gather.7.cloned.1.call-done = f32[128,128,128]{2,1,0:T(8,128)} async-done(((f32[8,128,128]{2,1,0:T(8,128)}), f32[128,128,128]{2,1,0:T(8,128)}) %all-gather.7.cloned.1.call-update) | async-done | bytes 8388624 | tf_op jit(solution)/shard_map/all_gather | solution.py:22
  301.7 105.9 %all-gather.9.cloned.1.call-done = f32[128,128,128]{2,1,0:T(8,128)} async-done(((f32[8,128,128]{2,1,0:T(8,128)}), f32[128,128,128]{2,1,0:T(8,128)}) %all-gather.9.cloned.1.call-update) | async-done | bytes 8388624 | tf_op jit(solution)/shard_map/all_gather | solution.py:22
  407.6 29.2 %while.41 = (s32[]{:T(128)}, f32[8,128,128]{2,1,0:T(8,128)S(1)}, s32[]{:T(128)}, f32[16,8,128,128]{3,2,1,0:T(8,128)}, f32[16,8,128,128]{3,2,1,0:T(8,128)}, /*index=5*/s32[]{:T(128)}, s32[]{:T(128)}) while((s32[]{:T(128)}, f32[8,128,128]{2,1,0:T(8,128)S(1)}, s32[]{:T(128)}, f32[16,8,128,128]{3,2,1,0:T(8,128)}, ...), condition=%wide.region_5.6_spmd.clone, body=%wide.region_4.5_spmd.clone.sunk | while | flops 201850880 | bytes 3672671 | solution.py:31
  407.6 1.9 fusion.97
  409.6 1.9 fusion.97
  411.5 1.9 fusion.97
  413.5 1.9 fusion.97
  415.4 1.9 fusion.97
  417.4 1.9 fusion.97
  419.3 1.9 fusion.97
  421.3 1.9 fusion.97
  423.2 1.9 fusion.97
  425.2 1.9 fusion.97
  427.1 1.9 fusion.97
  429.1 1.9 fusion.97
  431.0 1.9 fusion.97
  433.0 1.9 fusion.97
  434.9 1.9 fusion.97
  436.8 6.0 %while.39 = (s32[]{:T(128)}, f32[8,128,128]{2,1,0:T(8,128)S(1)}, f32[2,8,64,128]{3,2,1,0:T(8,128)}, f32[2,8,128,128]{3,2,1,0:T(8,128)S(1)}, f32[2,8,128,128]{3,2...) while((s32[]{:T(128)}, f32[8,128,128]{2,1,0:T(8,128)S(1)}, ...), condition=%wide.region_8.9_spmd, body=%wide.region_7.8_spmd.sunk | while | flops 302186496 | bytes 4458581 | solution.py:172
  436.9 2.3 fusion.89
  439.9 2.3 fusion.89
  442.8 1.3 multiply_reduce_fusion.1
  444.2 1.4 copy.105
  445.5 58.0 %all-gather.11.cloned.1.call-done = bf16[1,1024,2048]{2,1,0:T(8,128)(2,1)} async-done(((bf16[1,1024,128]{2,1,0:T(8,128)(2,1)}), bf16[1,1024,2048]{2,1,0:T(8,128)(2,1)}) %all-gather.11.cloned.1.call-update) | async-done | bytes 4194320 | tf_op jit(solution)/shard_map/all_gather | solution.py:178
  503.7 3.0 fusion.32
  506.7 1.9 collective-permute-start.1
  508.7 11.9 %collective-permute-done.1 = bf16[1,128,2048]{2,1,0:T(8,128)(2,1)S(1)} collective-permute-done((bf16[1,128,2048]{2,1,0:T(8,128)(2,1)S(1)}, bf16[1,128,2048]{2,1,0:T(8,128)(2,1)S(1)}, u32[]{:S(2)}, u32[]{:S(2)}) %collective-permute-start.1) | collective-permute-done | bytes 524320 | tf_op jit(solution)/shard_map/ppermute | solution.py:37
  520.5 0.8 copy.160
  (99 shorter events, 11.8 us)
Async XLA Ops:
  6.5 9.7 %copy-start.7 = (bf16[1,128,5120]{2,1,0:T(8,128)(2,1)S(1)}, bf16[1,128,5120]{2,1,0:T(8,128)(2,1)}, u32[]{:S(2)}) copy-start(bf16[1,128,5120]{2,1,0:T(8,128)(2,1)} %param.12) | copy-start | bytes 3932164
  6.5 295.1 %all-gather.7.cloned.1.call-start = ((), (), s32[]{:S(2)}) async-start(), calls=%async_computation | async-start | bytes 8912896 | tf_op jit(solution)/shard_map/all_gather | solution.py:22
  7.6 8.7 %collective-permute-start = (bf16[3,5120]{1,0:T(4,128)(2,1)S(1)}, bf16[3,5120]{1,0:T(4,128)(2,1)S(1)}, u32[]{:S(2)}, u32[]{:S(2)}) collective-permute-start(bf16[3,5120]{1,0:T(4,128)(2,1)S(1)} %slice_bitcast_fusion.3), channel_id=1, source_target_pairs={{0,1},{1,2},{2,3},{3,4},{4,5},{5,6},{6,7},{7,8},{8,9},{9,10},{10,1... | collective-permute-start | bytes 92168 | tf_op jit(solution)/shard_map/ppermute | solution.py:17
  18.1 1.5 copy-start.6
  21.0 168.3 %copy-start = (f32[8,128,2,128]{3,2,1,0:T(2,128)}, f32[8,128,2,128]{3,2,1,0:T(2,128)S(1)}, u32[]{:S(2)}) copy-start(f32[8,128,2,128]{3,2,1,0:T(2,128)S(1)} %copy.83) | copy-start | bytes 3145732
  183.0 1.9 copy-start.8
  186.9 2.3 copy-start.3
  194.5 0.8 copy-start.2
  194.5 1.0 copy-start.5
  195.4 212.2 %all-gather.9.cloned.1.call-start = ((), (), s32[]{:S(2)}) async-start(), calls=%async_computation.1 | async-start | bytes 8912896 | tf_op jit(solution)/shard_map/all_gather | solution.py:22
  196.1 307.4 %all-gather.11.cloned.1.call-start = ((), (), s32[]{:S(2)}) async-start(), calls=%async_computation.2 | async-start | bytes 4456448 | tf_op jit(solution)/shard_map/all_gather | solution.py:178
  197.1 1.9 copy-start.1
  198.5 2.7 copy-start.4
  436.8 66.9 %copy-start.9 = (f32[1,1024]{1,0:T(1,128)S(1)}, f32[1,1024]{1,0:T(1,128)}, u32[]{:S(2)}) copy-start(f32[1,1024]{1,0:T(1,128)} %param.16) | copy-start | bytes 12292
  506.7 13.8 %collective-permute-start.1 = (bf16[1,128,2048]{2,1,0:T(8,128)(2,1)S(1)}, bf16[1,128,2048]{2,1,0:T(8,128)(2,1)S(1)}, u32[]{:S(2)}, u32[]{:S(2)}) collective-permute-start(bf16[1,128,2048]{2,1,0:T(8,128)(2,1)S(1)} %fusion.32), channel_id=1, source_target_pairs={{0,16},{16,32},{32,48},{48,64},{64,80},{80,96},{96,112},{112,128},... | collective-permute-start | bytes 1572872 | tf_op jit(solution)/shard_map/ppermute | solution.py:37
Sparse Core Ops, SparseCore 0:
  195.5 106.1 all-gather.6
  303.8 103.7 all-gather.8
  409.6 93.8 all-gather.10
where the time goes:
time: 529 us; the launch traced here: 528 us
  waiting for transfers between devices  275 us (52%)
  other arithmetic  167 us (32%)
  matrix products  53.5 us (10%)
  between operations  13.6 us (3%)
  local copies, waits for them, and re-layouts  12.2 us (2%)
  starting transfers between devices  6.05 us (1%)
    all_gather x2, waiting for transfers between devices, entering(): pieces = jax.tree.map(lambda part: lax.all_gather(part, axis), value)  203 us
    another operation x2, other arithmetic, span_terms(): jax.scipy.linalg.solve_triangular(unit_lower, right_sides, lower=True, un...  158 us
    all_gather x1, waiting for transfers between devices, on_device(): lax.all_gather(local_cols, 'ctx', axis=1, tiled=True)  58 us
    dot_general x15, matrix products, combine_pairs(): jnp.einsum('hde,hef->hdf', second_map, first_add, precision=highest)  28.1 us
    ppermute x1, waiting for transfers between devices, passed_along(): return lax.ppermute(value, axis, pairs)  11.9 us
  transfers between devices with their start and end apart: 5, of which 5 were waited for; matrix products, arithmetic and copies ran while one was open for 9% of the time, Pallas kernels for 0%

commit v1 on v0

--- a/solution.py
+++ b/solution.py
@@ -9,6 +9,24 @@
 CONV = 4
 SPAN = 128
 highest = lax.Precision.HIGHEST
+
+
+def collect(value, axis, dim):
+    ways, here, step = (lax.axis_size(axis), lax.axis_index(axis), value.shape[dim])
+    shape = [n * ways if d == dim else n for d, n in enumerate(value.shape)]
+    full = lax.dynamic_update_slice_in_dim(
+        jnp.zeros(shape, value.dtype), value, here * step, axis=dim
+    )
+    going_up = going_down = value
+    for far in range(1, ways // 2 + 1):
+        going_up = lax.ppermute(going_up, axis, [(d, (d + 1) % ways) for d in range(ways)])
+        full = lax.dynamic_update_slice_in_dim(full, going_up, (here - far) % ways * step, axis=dim)
+        if 2 * far < ways:
+            going_down = lax.ppermute(going_down, axis, [(d, (d - 1) % ways) for d in range(ways)])
+            full = lax.dynamic_update_slice_in_dim(
+                full, going_down, (here + far) % ways * step, axis=dim
+            )
+    return full
 
 
 def shifted(value, axis, steps):
@@ -174,9 +192,7 @@
     normed = normalize(outputs, norm_gain[0])
     local_cols = w_out[0]
     mixed_rows = jnp.dot(
-        normed,
-        lax.all_gather(local_cols, "ctx", axis=1, tiled=True),
-        preferred_element_type=jnp.float32,
+        normed, collect(local_cols, "ctx", 1), preferred_element_type=jnp.float32
     ).astype(jnp.bfloat16)
     return passed_along(mixed_rows[None], "section", 1)
 

time: 529 us -> 512 us (0.968)
  the two profiles are of different devices: /device:TPU:32 before, /device:TPU:8 now
where the time goes in v1:
time: 512 us; the launch traced here: 511 us
  waiting for transfers between devices  187 us (37%)
  other arithmetic  167 us (33%)
  starting transfers between devices  60.5 us (12%)
  matrix products  53.4 us (10%)
  local copies, waits for them, and re-layouts  27.7 us (5%)
  between operations  14.4 us (3%)
    another operation x2, other arithmetic, span_terms(): jax.scipy.linalg.solve_triangular(unit_lower, right_sides, lower=True, un...  158 us
    all_gather x2, waiting for transfers between devices, entering(): pieces = jax.tree.map(lambda part: lax.all_gather(part, axis), value)  125 us
    ppermute x8, waiting for transfers between devices, collect(): lax.ppermute(going_up, axis, [(d, (d + 1) % ways) for d in range(ways)])  47.5 us
    ppermute x7, starting transfers between devices, collect(): lax.ppermute(going_down, axis, [(d, (d - 1) % ways) for d in range(ways)])  37.2 us
    dot_general x15, matrix products, combine_pairs(): jnp.einsum('hde,hef->hdf', second_map, first_add, precision=highest)  28.1 us
    ppermute x8, starting transfers between devices, collect(): lax.ppermute(going_up, axis, [(d, (d + 1) % ways) for d in range(ways)])  17.6 us
    ppermute x1, waiting for transfers between devices, passed_along(): return lax.ppermute(value, axis, pairs)  10.7 us
  transfers between devices with their start and end apart: 19, of which 15 were waited for; matrix products, arithmetic and copies ran while one was open for 5% of the time, Pallas kernels for 0%

profile of v1, /device:TPU:8, one launch (start us, length us, event | category | flops | bytes accessed | tf_op | source)
XLA Modules:
  0.0 510.5 jit_solution(17492314483921267301)
XLA Ops:
  7.6 3.8 collective-permute-start
  22.1 2.4 fusion.36
  24.5 157.9 %custom-call.4 = f32[8,2,1,128,128]{3,4,2,1,0:T(8,128)} custom-call(f32[8,2,1,128,128]{4,3,2,1,0:T(8,128)S(1)} %fusion.36), custom_call_target="InvertDiagBlocksLowerTriangular" | custom-call | tf_op jit(solution)/shard_map/jit(_solve_triangular)/vmap(vmap())/triangular_solve | solution.py:119
  182.4 1.9 broadcast_multiply_fusion
  184.3 2.0 fusion.28
  186.3 2.2 convolution_bitcast_fusion
  188.5 2.2 fusion.32
  191.0 2.8 while.40
  195.5 3.8 collective-permute-start.1
  199.3 7.3 %collective-permute-start.2 = (bf16[1024,128]{1,0:T(8,128)(2,1)S(1)}, bf16[1024,128]{1,0:T(8,128)(2,1)}, u32[]{:S(2)}, u32[]{:S(2)}) collective-permute-start(bf16[1024,128]{1,0:T(8,128)(2,1)S(1)} %bitcast.169), channel_id=1, source_target_pairs={{0,15},{1,0},{2,1},{3,2},{4,3},{5,4},{6,5},{7,6},{8,7},{9,8},{10,9... | collective-permute-start | bytes 786440 | tf_op jit(solution)/shard_map/ppermute | solution.py:25
  207.3 2.5 broadcast_in_dim.67
  212.4 2.1 collective-permute-start.3
  214.5 2.1 convolution_multiply_fusion.1
  216.6 5.1 %collective-permute-start.4 = (bf16[1024,128]{1,0:T(8,128)(2,1)}, bf16[1024,128]{1,0:T(8,128)(2,1)S(1)}, u32[]{:S(2)}, u32[]{:S(2)}) collective-permute-start(bf16[1024,128]{1,0:T(8,128)(2,1)} %collective-permute-done.2), channel_id=1, source_target_pairs={{0,15},{1,0},{2,1},{3,2},{4,3},{5,4},{6,5},{7,6},{8,7},{9,8},{10,9... | collective-permute-start | bytes 786440 | tf_op jit(solution)/shard_map/ppermute | solution.py:25
  221.8 6.9 %collective-permute-done.3 = bf16[1024,128]{1,0:T(8,128)(2,1)S(1)} collective-permute-done((bf16[1024,128]{1,0:T(8,128)(2,1)S(1)}, bf16[1024,128]{1,0:T(8,128)(2,1)S(1)}, u32[]{:S(2)}, u32[]{:S(2)}) %collective-permute-start.3) | collective-permute-done | bytes 262176 | tf_op jit(solution)/shard_map/ppermute | solution.py:22
  228.6 2.1 collective-permute-start.5
  233.0 4.8 collective-permute-start.6
  237.7 7.0 %collective-permute-done.5 = bf16[1024,128]{1,0:T(8,128)(2,1)S(1)} collective-permute-done((bf16[1024,128]{1,0:T(8,128)(2,1)S(1)}, bf16[1024,128]{1,0:T(8,128)(2,1)S(1)}, u32[]{:S(2)}, u32[]{:S(2)}) %collective-permute-start.5) | collective-permute-done | bytes 262176 | tf_op jit(solution)/shard_map/ppermute | solution.py:22
  244.7 1.9 collective-permute-start.7
  246.6 1.9 convolution_bitcast_fusion.2
  249.3 5.1 %collective-permute-start.8 = (bf16[1024,128]{1,0:T(8,128)(2,1)S(1)}, bf16[1024,128]{1,0:T(8,128)(2,1)S(1)}, u32[]{:S(2)}, u32[]{:S(2)}) collective-permute-start(bf16[1024,128]{1,0:T(8,128)(2,1)S(1)} %collective-permute-done.6), channel_id=1, source_target_pairs={{0,15},{1,0},{2,1},{3,2},{4,3},{5,4},{6,5},{7,6},{8,7},{9,8},{10,9... | collective-permute-start | bytes 786440 | tf_op jit(solution)/shard_map/ppermute | solution.py:25
  256.1 4.5 collective-permute-done.7
  260.6 1.9 collective-permute-start.9
  264.9 5.0 collective-permute-start.10
  270.7 5.9 %collective-permute-done.9 = bf16[1024,128]{1,0:T(8,128)(2,1)S(1)} collective-permute-done((bf16[1024,128]{1,0:T(8,128)(2,1)S(1)}, bf16[1024,128]{1,0:T(8,128)(2,1)S(1)}, u32[]{:S(2)}, u32[]{:S(2)}) %collective-permute-start.9) | collective-permute-done | bytes 262176 | tf_op jit(solution)/shard_map/ppermute | solution.py:22
  276.6 1.9 collective-permute-start.11
  280.3 5.1 %collective-permute-start.12 = (bf16[1024,128]{1,0:T(8,128)(2,1)S(1)}, bf16[1024,128]{1,0:T(8,128)(2,1)S(1)}, u32[]{:S(2)}, u32[]{:S(2)}) collective-permute-start(bf16[1024,128]{1,0:T(8,128)(2,1)S(1)} %collective-permute-done.10), channel_id=1, source_target_pairs={{0,15},{1,0},{2,1},{3,2},{4,3},{5,4},{6,5},{7,6},{8,7},{9,8},{10,9... | collective-permute-start | bytes 786440 | tf_op jit(solution)/shard_map/ppermute | solution.py:25
  286.2 6.3 %collective-permute-done.11 = bf16[1024,128]{1,0:T(8,128)(2,1)S(1)} collective-permute-done((bf16[1024,128]{1,0:T(8,128)(2,1)S(1)}, bf16[1024,128]{1,0:T(8,128)(2,1)S(1)}, u32[]{:S(2)}, u32[]{:S(2)}) %collective-permute-start.11) | collective-permute-done | bytes 262176 | tf_op jit(solution)/shard_map/ppermute | solution.py:22
  292.5 1.9 collective-permute-start.13
  296.3 4.7 collective-permute-start.14
  301.8 6.6 %collective-permute-done.13 = bf16[1024,128]{1,0:T(8,128)(2,1)S(1)} collective-permute-done((bf16[1024,128]{1,0:T(8,128)(2,1)S(1)}, bf16[1024,128]{1,0:T(8,128)(2,1)S(1)}, u32[]{:S(2)}, u32[]{:S(2)}) %collective-permute-start.13) | collective-permute-done | bytes 262176 | tf_op jit(solution)/shard_map/ppermute | solution.py:22
  308.4 1.9 collective-permute-start.15
  313.2 10.4 %collective-permute-done.15 = bf16[1024,128]{1,0:T(8,128)(2,1)S(1)} collective-permute-done((bf16[1024,128]{1,0:T(8,128)(2,1)S(1)}, bf16[1024,128]{1,0:T(8,128)(2,1)S(1)}, u32[]{:S(2)}, u32[]{:S(2)}) %collective-permute-start.15) | collective-permute-done | bytes 262176 | tf_op jit(solution)/shard_map/ppermute | solution.py:22
  324.4 17.6 %all-gather.7.cloned.1.call-done = f32[128,128,128]{2,1,0:T(8,128)} async-done(((f32[8,128,128]{2,1,0:T(8,128)}), f32[128,128,128]{2,1,0:T(8,128)}) %all-gather.7.cloned.1.call-update) | async-done | bytes 8388624 | tf_op jit(solution)/shard_map/all_gather | solution.py:40
  342.0 107.2 %all-gather.5.cloned.1.call-done = f32[128,128,128]{2,1,0:T(8,128)} async-done(((f32[8,128,128]{2,1,0:T(8,128)}), f32[128,128,128]{2,1,0:T(8,128)}) %all-gather.5.cloned.1.call-update) | async-done | bytes 8388624 | tf_op jit(solution)/shard_map/all_gather | solution.py:40
  449.2 29.2 %while.41 = (s32[]{:T(128)}, f32[8,128,128]{2,1,0:T(8,128)S(1)}, s32[]{:T(128)}, f32[16,8,128,128]{3,2,1,0:T(8,128)}, f32[16,8,128,128]{3,2,1,0:T(8,128)}, /*index=5*/s32[]{:T(128)}, s32[]{:T(128)}) while((s32[]{:T(128)}, f32[8,128,128]{2,1,0:T(8,128)S(1)}, s32[]{:T(128)}, f32[16,8,128,128]{3,2,1,0:T(8,128)}, ...), condition=%wide.region_5.6_spmd.clone, body=%wide.region_4.5_spmd.clone.sunk | while | flops 201850880 | bytes 3672679 | solution.py:49
  449.2 1.9 fusion.91
  453.1 1.9 fusion.91
  455.0 1.9 fusion.91
  457.0 1.9 fusion.91
  458.9 1.9 fusion.91
  470.6 1.9 fusion.91
  478.4 6.0 %while.39 = (s32[]{:T(128)}, f32[8,128,128]{2,1,0:T(8,128)S(1)}, f32[2,8,64,128]{3,2,1,0:T(8,128)}, f32[2,8,128,128]{3,2,1,0:T(8,128)S(1)}, f32[2,8,128,128]{3,2...) while((s32[]{:T(128)}, f32[8,128,128]{2,1,0:T(8,128)S(1)}, ...), condition=%wide.region_8.9_spmd, body=%wide.region_7.8_spmd.sunk | while | flops 302186496 | bytes 4458589 | solution.py:190
  478.4 2.3 fusion.83
  481.4 2.3 fusion.83
  487.3 3.0 fusion.27
  490.3 1.9 collective-permute-start.16
  492.2 10.7 %collective-permute-done.16 = bf16[1,128,2048]{2,1,0:T(8,128)(2,1)S(1)} collective-permute-done((bf16[1,128,2048]{2,1,0:T(8,128)(2,1)S(1)}, bf16[1,128,2048]{2,1,0:T(8,128)(2,1)S(1)}, u32[]{:S(2)}, u32[]{:S(2)}) %collective-permute-start.16) | collective-permute-done | bytes 524320 | tf_op jit(solution)/shard_map/ppermute | solution.py:55
  (149 shorter events, 58.1 us)
Async XLA Ops:
  6.5 9.1 %copy-start.7 = (bf16[1,128,5120]{2,1,0:T(8,128)(2,1)S(1)}, bf16[1,128,5120]{2,1,0:T(8,128)(2,1)}, u32[]{:S(2)}) copy-start(bf16[1,128,5120]{2,1,0:T(8,128)(2,1)} %param.12) | copy-start | bytes 3932164
  6.5 335.4 %all-gather.7.cloned.1.call-start = ((), (), s32[]{:S(2)}) async-start(), calls=%async_computation.1 | async-start | bytes 8912896 | tf_op jit(solution)/shard_map/all_gather | solution.py:40
  7.6 8.1 %collective-permute-start = (bf16[3,5120]{1,0:T(4,128)(2,1)S(1)}, bf16[3,5120]{1,0:T(4,128)(2,1)S(1)}, u32[]{:S(2)}, u32[]{:S(2)}) collective-permute-start(bf16[3,5120]{1,0:T(4,128)(2,1)S(1)} %slice_bitcast_fusion.3), channel_id=1, source_target_pairs={{0,1},{1,2},{2,3},{3,4},{4,5},{5,6},{6,7},{7,8},{8,9},{9,10},{10,1... | collective-permute-start | bytes 92168 | tf_op jit(solution)/shard_map/ppermute | solution.py:35
  17.5 1.5 copy-start.6
  22.1 166.4 %copy-start = (f32[8,128,2,128]{3,2,1,0:T(2,128)}, f32[8,128,2,128]{3,2,1,0:T(2,128)S(1)}, u32[]{:S(2)}) copy-start(f32[8,128,2,128]{3,2,1,0:T(2,128)S(1)} %copy.83) | copy-start | bytes 3145732
  182.4 1.9 copy-start.8
  186.3 4.5 copy-start.3
  191.0 4.4 copy-start.9
  193.8 0.8 copy-start.5
  193.9 1.0 copy-start.2
  194.7 254.5 %all-gather.5.cloned.1.call-start = ((), (), s32[]{:S(2)}) async-start(), calls=%async_computation | async-start | bytes 8912896 | tf_op jit(solution)/shard_map/all_gather | solution.py:40
  195.5 16.9 %collective-permute-start.1 = (bf16[1024,128]{1,0:T(8,128)(2,1)S(1)}, bf16[1024,128]{1,0:T(8,128)(2,1)S(1)}, u32[]{:S(2)}, u32[]{:S(2)}) collective-permute-start(bf16[1024,128]{1,0:T(8,128)(2,1)S(1)} %bitcast.168), channel_id=1, source_target_pairs={{0,1},{1,2},{2,3},{3,4},{4,5},{5,6},{6,7},{7,8},{8,9},{9,10},{10,1... | collective-permute-start | bytes 786440 | tf_op jit(solution)/shard_map/ppermute | solution.py:22
  199.3 17.3 %collective-permute-start.2 = (bf16[1024,128]{1,0:T(8,128)(2,1)S(1)}, bf16[1024,128]{1,0:T(8,128)(2,1)}, u32[]{:S(2)}, u32[]{:S(2)}) collective-permute-start(bf16[1024,128]{1,0:T(8,128)(2,1)S(1)} %bitcast.169), channel_id=1, source_target_pairs={{0,15},{1,0},{2,1},{3,2},{4,3},{5,4},{6,5},{7,6},{8,7},{9,8},{10,9... | collective-permute-start | bytes 786440 | tf_op jit(solution)/shard_map/ppermute | solution.py:25
  210.5 3.9 copy-start.1
  211.8 19.0 %copy-start.4 = (f32[8,2,128,256]{3,2,1,0:T(8,128)S(1)}, f32[8,2,128,256]{3,2,1,0:T(8,128)}, u32[]{:S(2)}) copy-start(f32[8,2,128,256]{3,2,1,0:T(8,128)} %copy-done.3) | copy-start | bytes 6291460
  212.4 16.2 %copy-start.10 = (bf16[1024,128]{1,0:T(8,128)(2,1)}, bf16[1024,128]{1,0:T(8,128)(2,1)S(1)}, u32[]{:S(2)}) copy-start(bf16[1024,128]{1,0:T(8,128)(2,1)S(1)} %collective-permute-done.1) | copy-start | bytes 786436
  212.4 16.2 %collective-permute-start.3 = (bf16[1024,128]{1,0:T(8,128)(2,1)S(1)}, bf16[1024,128]{1,0:T(8,128)(2,1)S(1)}, u32[]{:S(2)}, u32[]{:S(2)}) collective-permute-start(bf16[1024,128]{1,0:T(8,128)(2,1)S(1)} %collective-permute-done.1), channel_id=1, source_target_pairs={{0,1},{1,2},{2,3},{3,4},{4,5},{5,6},{6,7},{7,8},{8,9},{9,10},{10,1... | collective-permute-start | bytes 786440 | tf_op jit(solution)/shard_map/ppermute | solution.py:22
  216.6 16.4 %collective-permute-start.4 = (bf16[1024,128]{1,0:T(8,128)(2,1)}, bf16[1024,128]{1,0:T(8,128)(2,1)S(1)}, u32[]{:S(2)}, u32[]{:S(2)}) collective-permute-start(bf16[1024,128]{1,0:T(8,128)(2,1)} %collective-permute-done.2), channel_id=1, source_target_pairs={{0,15},{1,0},{2,1},{3,2},{4,3},{5,4},{6,5},{7,6},{8,7},{9,8},{10,9... | collective-permute-start | bytes 786440 | tf_op jit(solution)/shard_map/ppermute | solution.py:25
  228.6 16.1 %collective-permute-start.5 = (bf16[1024,128]{1,0:T(8,128)(2,1)S(1)}, bf16[1024,128]{1,0:T(8,128)(2,1)S(1)}, u32[]{:S(2)}, u32[]{:S(2)}) collective-permute-start(bf16[1024,128]{1,0:T(8,128)(2,1)S(1)} %collective-permute-done.3), channel_id=1, source_target_pairs={{0,1},{1,2},{2,3},{3,4},{4,5},{5,6},{6,7},{7,8},{8,9},{9,10},{10,1... | collective-permute-start | bytes 786440 | tf_op jit(solution)/shard_map/ppermute | solution.py:22
  230.8 17.8 %copy-start.11 = (bf16[1024,128]{1,0:T(8,128)(2,1)S(1)}, bf16[1024,128]{1,0:T(8,128)(2,1)}, u32[]{:S(2)}) copy-start(bf16[1024,128]{1,0:T(8,128)(2,1)} %copy-done.10) | copy-start | bytes 786436
  233.0 16.3 %collective-permute-start.6 = (bf16[1024,128]{1,0:T(8,128)(2,1)S(1)}, bf16[1024,128]{1,0:T(8,128)(2,1)S(1)}, u32[]{:S(2)}, u32[]{:S(2)}) collective-permute-start(bf16[1024,128]{1,0:T(8,128)(2,1)S(1)} %collective-permute-done.4), channel_id=1, source_target_pairs={{0,15},{1,0},{2,1},{3,2},{4,3},{5,4},{6,5},{7,6},{8,7},{9,8},{10,9... | collective-permute-start | bytes 786440 | tf_op jit(solution)/shard_map/ppermute | solution.py:25
  244.7 15.9 %collective-permute-start.7 = (bf16[1024,128]{1,0:T(8,128)(2,1)S(1)}, bf16[1024,128]{1,0:T(8,128)(2,1)S(1)}, u32[]{:S(2)}, u32[]{:S(2)}) collective-permute-start(bf16[1024,128]{1,0:T(8,128)(2,1)S(1)} %collective-permute-done.5), channel_id=1, source_target_pairs={{0,1},{1,2},{2,3},{3,4},{4,5},{5,6},{6,7},{7,8},{8,9},{9,10},{10,1... | collective-permute-start | bytes 786440 | tf_op jit(solution)/shard_map/ppermute | solution.py:22
  249.3 15.6 %collective-permute-start.8 = (bf16[1024,128]{1,0:T(8,128)(2,1)S(1)}, bf16[1024,128]{1,0:T(8,128)(2,1)S(1)}, u32[]{:S(2)}, u32[]{:S(2)}) collective-permute-start(bf16[1024,128]{1,0:T(8,128)(2,1)S(1)} %collective-permute-done.6), channel_id=1, source_target_pairs={{0,15},{1,0},{2,1},{3,2},{4,3},{5,4},{6,5},{7,6},{8,7},{9,8},{10,9... | collective-permute-start | bytes 786440 | tf_op jit(solution)/shard_map/ppermute | solution.py:25
  260.6 15.9 %collective-permute-start.9 = (bf16[1024,128]{1,0:T(8,128)(2,1)S(1)}, bf16[1024,128]{1,0:T(8,128)(2,1)S(1)}, u32[]{:S(2)}, u32[]{:S(2)}) collective-permute-start(bf16[1024,128]{1,0:T(8,128)(2,1)S(1)} %collective-permute-done.7), channel_id=1, source_target_pairs={{0,1},{1,2},{2,3},{3,4},{4,5},{5,6},{6,7},{7,8},{8,9},{9,10},{10,1... | collective-permute-start | bytes 786440 | tf_op jit(solution)/shard_map/ppermute | solution.py:22
  264.9 15.4 %collective-permute-start.10 = (bf16[1024,128]{1,0:T(8,128)(2,1)S(1)}, bf16[1024,128]{1,0:T(8,128)(2,1)S(1)}, u32[]{:S(2)}, u32[]{:S(2)}) collective-permute-start(bf16[1024,128]{1,0:T(8,128)(2,1)S(1)} %collective-permute-done.8), channel_id=1, source_target_pairs={{0,15},{1,0},{2,1},{3,2},{4,3},{5,4},{6,5},{7,6},{8,7},{9,8},{10,9... | collective-permute-start | bytes 786440 | tf_op jit(solution)/shard_map/ppermute | solution.py:25
  276.6 15.9 %collective-permute-start.11 = (bf16[1024,128]{1,0:T(8,128)(2,1)S(1)}, bf16[1024,128]{1,0:T(8,128)(2,1)S(1)}, u32[]{:S(2)}, u32[]{:S(2)}) collective-permute-start(bf16[1024,128]{1,0:T(8,128)(2,1)S(1)} %collective-permute-done.9), channel_id=1, source_target_pairs={{0,1},{1,2},{2,3},{3,4},{4,5},{5,6},{6,7},{7,8},{8,9},{9,10},{10,1... | collective-permute-start | bytes 786440 | tf_op jit(solution)/shard_map/ppermute | solution.py:22
  280.3 16.0 %collective-permute-start.12 = (bf16[1024,128]{1,0:T(8,128)(2,1)S(1)}, bf16[1024,128]{1,0:T(8,128)(2,1)S(1)}, u32[]{:S(2)}, u32[]{:S(2)}) collective-permute-start(bf16[1024,128]{1,0:T(8,128)(2,1)S(1)} %collective-permute-done.10), channel_id=1, source_target_pairs={{0,15},{1,0},{2,1},{3,2},{4,3},{5,4},{6,5},{7,6},{8,7},{9,8},{10,9... | collective-permute-start | bytes 786440 | tf_op jit(solution)/shard_map/ppermute | solution.py:25
  292.5 15.9 %collective-permute-start.13 = (bf16[1024,128]{1,0:T(8,128)(2,1)S(1)}, bf16[1024,128]{1,0:T(8,128)(2,1)S(1)}, u32[]{:S(2)}, u32[]{:S(2)}) collective-permute-start(bf16[1024,128]{1,0:T(8,128)(2,1)S(1)} %collective-permute-done.11), channel_id=1, source_target_pairs={{0,1},{1,2},{2,3},{3,4},{4,5},{5,6},{6,7},{7,8},{8,9},{9,10},{10,1... | collective-permute-start | bytes 786440 | tf_op jit(solution)/shard_map/ppermute | solution.py:22
  296.3 16.1 %collective-permute-start.14 = (bf16[1024,128]{1,0:T(8,128)(2,1)S(1)}, bf16[1024,128]{1,0:T(8,128)(2,1)S(1)}, u32[]{:S(2)}, u32[]{:S(2)}) collective-permute-start(bf16[1024,128]{1,0:T(8,128)(2,1)S(1)} %collective-permute-done.12), channel_id=1, source_target_pairs={{0,15},{1,0},{2,1},{3,2},{4,3},{5,4},{6,5},{7,6},{8,7},{9,8},{10,9... | collective-permute-start | bytes 786440 | tf_op jit(solution)/shard_map/ppermute | solution.py:25
  308.4 15.2 %collective-permute-start.15 = (bf16[1024,128]{1,0:T(8,128)(2,1)S(1)}, bf16[1024,128]{1,0:T(8,128)(2,1)S(1)}, u32[]{:S(2)}, u32[]{:S(2)}) collective-permute-start(bf16[1024,128]{1,0:T(8,128)(2,1)S(1)} %collective-permute-done.13), channel_id=1, source_target_pairs={{0,1},{1,2},{2,3},{3,4},{4,5},{5,6},{6,7},{7,8},{8,9},{9,10},{10,1... | collective-permute-start | bytes 786440 | tf_op jit(solution)/shard_map/ppermute | solution.py:22
  478.3 8.9 %copy-start.12 = (f32[1,1024]{1,0:T(1,128)S(1)}, f32[1,1024]{1,0:T(1,128)}, u32[]{:S(2)}) copy-start(f32[1,1024]{1,0:T(1,128)} %param.16) | copy-start | bytes 12292
  490.3 12.6 %collective-permute-start.16 = (bf16[1,128,2048]{2,1,0:T(8,128)(2,1)S(1)}, bf16[1,128,2048]{2,1,0:T(8,128)(2,1)S(1)}, u32[]{:S(2)}, u32[]{:S(2)}) collective-permute-start(bf16[1,128,2048]{2,1,0:T(8,128)(2,1)S(1)} %fusion.27), channel_id=1, source_target_pairs={{0,16},{16,32},{32,48},{48,64},{64,80},{80,96},{96,112},{112,128},... | collective-permute-start | bytes 1572872 | tf_op jit(solution)/shard_map/ppermute | solution.py:55
Sparse Core Ops, SparseCore 0:
  194.8 147.0 all-gather.6
  344.0 105.0 all-gather.4
